TPU v7x, 512 devices: a whole 4x4x16 slice. The times are simulated.
512 devices in a mesh: prow: 16 (over x, y), pcol: 32 (over z, core).
Axes of the slice: x: 4, y: 4, z: 16, core: 2. Of those that a mesh axis runs over, the one named last changes fastest.
Arguments:
- adjoint_trail: float32 [2, 16, 256, 1, 32, 256], P(None, 'prow', None, None, 'pcol'), as said below
- factor_low: float32 [2, 16, 32, 8, 4, 256], P(None, 'prow', 'pcol'), may hold values from -0.0625 to 0.0625
- adjoint_low: float32 [2, 16, 32, 8, 4, 256], P(None, 'prow', 'pcol'), may hold values from -6 to 6
- factor_top: float32 [10, 256, 256], P(None, 'pcol'), as said below
- adjoint_top: float32 [10, 256, 256], P(None, 'pcol'), may hold values from -6 to 6
- diag_inverse: float32 [4, 256, 256], P(None, 'pcol'), as said below
Outputs:
- grad_low: float32 [2, 16, 32, 8, 4, 256], P(None, 'prow', 'pcol')
- grad_top: float32 [10, 256, 256], P(None, 'pcol')
Inputs may be any that keep to these rules, and one draw needn't show every extreme that they name: adjoint_trail reshaped row-major to 8192 x 8192 is symmetric. The diagonal blocks factor_top[j (j + 1) / 2 + j] are lower triangular with a positive diagonal. diag_inverse[j] is the inverse of factor_top[j (j + 1) / 2 + j].
All inputs are finite; a program needn't handle non-finite values.
Results may differ from a plain program's by a relative error of at most 0.00024.
Values sent between devices are 32-bit elements; how exact they have to be, the bound alone decides.
A program may use at most 64 MiB of HBM per device.

v0:
```python
import jax
import jax.numpy as jnp
from jax import lax
from jax.sharding import PartitionSpec as P

NB = 256
K = 4
HIGHEST = lax.Precision.HIGHEST


def from_root(array, axis, root):
    mine = lax.axis_index(axis) == root
    return lax.psum(jnp.where(mine, array, jnp.zeros_like(array)), axis)


def matmul(left, right):
    return jnp.dot(left, right, precision=HIGHEST, preferred_element_type=jnp.float32)


def inner_product(left, right):
    return lax.dot_general(
        left, right, (((0,), (0,)), ((), ())), precision=HIGHEST, preferred_element_type=jnp.float32
    )


def block_slot(row_block, col_block):
    return row_block * (row_block + 1) // 2 + col_block


def half_lower(square):
    size = square.shape[0]
    row_ids = lax.broadcasted_iota(jnp.int32, (size, size), 0)
    col_ids = lax.broadcasted_iota(jnp.int32, (size, size), 1)
    return jnp.where(row_ids > col_ids, square, jnp.where(row_ids == col_ids, 0.5 * square, 0.0))


def diagonal_adjoint(diagonal, inverse, lower_adj):
    inner = half_lower(inner_product(jnp.tril(diagonal), lower_adj))
    spread = inner_product(inverse, matmul(inner, inverse))
    return 0.5 * (spread + spread.T)


def rows_one(piece):
    return lax.all_gather(piece, "pcol", axis=1, tiled=True)


def owner_one(piece, root):
    return from_root(piece, "prow", root)


def reduce_one(term, count):
    return lax.psum_scatter(
        term(jnp.int32(0), lax.axis_size("pcol") * count), "pcol", scatter_dimension=0, tiled=True
    )


def trailing_product(trail, panels, gather_rows, send_owner, reduce_rows):
    prow_count = lax.axis_size("prow")
    pcol_count = lax.axis_size("pcol")
    cycles, sub_rows, width = panels.shape
    block = sub_rows * pcol_count
    gathered = gather_rows(panels[:, None]).reshape(cycles, block, width)
    column = lax.axis_index("pcol")
    col_cycles = trail.shape[3]
    global_block = 0 + column
    share = lax.dynamic_index_in_dim(gathered, global_block // prow_count, 0, keepdims=False)
    owned = [send_owner(share, global_block % prow_count)]
    stacked = jnp.stack(owned)
    view = trail.reshape(cycles, pcol_count, sub_rows, col_cycles, block)
    unit = cycles * sub_rows

    def term(start, count):
        product = jnp.einsum(
            "iaekb,kbn->aien", view, stacked, precision=HIGHEST, preferred_element_type=jnp.float32
        )
        return product.reshape(count, width)

    return reduce_rows(term, unit).reshape(cycles, sub_rows, width)


def per_device(adjoint_trail, factor_low, adjoint_low, factor_top, adjoint_top, diag_inverse):
    cycles = factor_low.shape[0]
    sub_rows = factor_low.shape[3]
    local_rows = cycles * sub_rows
    low_factor = factor_low.reshape(cycles, sub_rows, K * NB)
    low_adjoint = adjoint_low.reshape(local_rows, K, NB)
    columns = low_factor.reshape(local_rows, K, NB)
    top_factor, top_adjoint, inverses = (
        lax.all_gather(factor_top, "pcol", axis=1, tiled=True),
        lax.all_gather(adjoint_top, "pcol", axis=1, tiled=True),
        lax.all_gather(diag_inverse, "pcol", axis=1, tiled=True),
    )
    lower_grads = [None] * K
    diag_grads = [None] * K
    upper_grads = {}
    grams = {}

    def lower_step(panel):
        single = low_factor[:, :, panel * NB : (panel + 1) * NB]
        image = trailing_product(adjoint_trail, single, rows_one, owner_one, reduce_one).reshape(
            local_rows, NB
        )
        residual = low_adjoint[:, panel] - 2.0 * image
        for later in range(panel + 1, K):
            residual = residual - matmul(lower_grads[later], top_factor[block_slot(later, panel)])
        lower_grads[panel] = matmul(residual, inverses[panel])

    def top_step(panel):
        for row_block in range(panel + 1, K):
            top_residual = top_adjoint[block_slot(row_block, panel)] - grams[row_block, panel]
            top_residual = top_residual - 2.0 * matmul(
                diag_grads[row_block], top_factor[block_slot(row_block, panel)]
            )
            for middle in range(panel + 1, row_block):
                top_residual = top_residual - matmul(
                    upper_grads[middle, row_block], top_factor[block_slot(middle, panel)]
                )
            for beyond in range(row_block + 1, K):
                top_residual = top_residual - inner_product(
                    upper_grads[row_block, beyond], top_factor[block_slot(beyond, panel)]
                )
            upper_grads[panel, row_block] = matmul(top_residual, inverses[panel])
        lower_adj = top_adjoint[block_slot(panel, panel)] - grams[panel, panel]
        for row_block in range(panel + 1, K):
            lower_adj = lower_adj - inner_product(
                upper_grads[panel, row_block], top_factor[block_slot(row_block, panel)]
            )
        diag_grads[panel] = diagonal_adjoint(
            top_factor[block_slot(panel, panel)], inverses[panel], jnp.tril(lower_adj)
        )

    for panel in reversed(range(K)):
        lower_step(panel)
        local_gram = jnp.stack(
            [inner_product(lower_grads[panel], columns[:, earlier]) for earlier in range(panel + 1)]
        )
        summed = lax.psum(local_gram, ("prow", "pcol"))
        for earlier in range(panel + 1):
            grams[panel, earlier] = summed[earlier]
        top_step(panel)
    grad_low = jnp.stack(lower_grads, 1).reshape(factor_low.shape)
    blocks = []
    for row_block in range(K):
        for col_block in range(row_block + 1):
            if row_block == col_block:
                blocks.append(diag_grads[col_block])
            else:
                blocks.append(upper_grads[col_block, row_block])
    full_top = jnp.stack(blocks)
    share_rows = factor_top.shape[1]
    grad_top = lax.dynamic_slice_in_dim(
        full_top, lax.axis_index("pcol") * share_rows, share_rows, 1
    )
    return (grad_low, grad_top)


def solution(mesh):
    in_specs = (
        P(None, "prow", None, None, "pcol", None),
        P(None, "prow", "pcol", None, None, None),
        P(None, "prow", "pcol", None, None, None),
        P(None, "pcol", None),
        P(None, "pcol", None),
        P(None, "pcol", None),
    )
    out_specs = (P(None, "prow", "pcol", None, None, None), P(None, "pcol", None))
    return jax.shard_map(
        per_device, mesh=mesh, in_specs=in_specs, out_specs=out_specs, check_vma=False
    )
```

profile of v0, /device:TPU:8, one launch (start us, length us, event | category | flops | bytes accessed | tf_op | source)
XLA Modules:
  0.0 1294.8 jit_solution(6312719842912323253)
XLA Ops:
  9.0 37.8 %all-gather.3 = f32[2,256,256]{2,1,0:T(8,128)S(1)} all-gather(f32[2,8,256]{2,1,0:T(8,128)S(1)} %get-tuple-element.15), channel_id=5, replica_groups=mesh['prow'=16,'pcol'=32] {'pcol'}, dimensions={1}, use_global_device_ids=true | all-gather | bytes 540672 | tf_op jit(solution)/shard_map/all_gather | solution.py:44
  46.8 28.5 %all-gather.2 = f32[2,256,256]{2,1,0:T(8,128)S(1)} all-gather(f32[2,8,256]{2,1,0:T(8,128)S(1)} %get-tuple-element.16), channel_id=4, replica_groups=mesh['prow'=16,'pcol'=32] {'pcol'}, dimensions={1}, use_global_device_ids=true | all-gather | bytes 540672 | tf_op jit(solution)/shard_map/all_gather | solution.py:44
  76.7 29.8 %all-gather.1 = f32[2,256,256]{2,1,0:T(8,128)S(1)} all-gather(f32[2,8,256]{2,1,0:T(8,128)S(1)} %get-tuple-element.17), channel_id=3, replica_groups=mesh['prow'=16,'pcol'=32] {'pcol'}, dimensions={1}, use_global_device_ids=true | all-gather | bytes 540672 | tf_op jit(solution)/shard_map/all_gather | solution.py:44
  107.3 28.5 %all-gather = f32[2,256,256]{2,1,0:T(8,128)S(1)} all-gather(f32[2,8,256]{2,1,0:T(8,128)S(1)} %get-tuple-element.14), channel_id=2, replica_groups=mesh['prow'=16,'pcol'=32] {'pcol'}, dimensions={1}, use_global_device_ids=true | all-gather | bytes 540672 | tf_op jit(solution)/shard_map/all_gather | solution.py:44
  137.2 113.6 %all-reduce.7.cloned.1.call-done = (f32[256,256]{1,0:T(8,128)}, f32[256,256]{1,0:T(8,128)}, f32[256,256]{1,0:T(8,128)}, f32[256,256]{1,0:T(8,128)}) async-done(((f32[256,256]{1,0:T(8,128)}, f32[256,256]{1,0:T(8,128)}, f32[256,256]{1,0:T(8,128)}, f32[256,256]{1,0:T(8,128)}), (f32[256,256]{1,0:T(8,128)}, f32[256,256]{1,0:T(8,128)}, f32[256,256]{1,0:T(8,128)}, ...) | async-done | bytes 1048592 | tf_op jit(solution)/shard_map/psum | solution.py:13
  250.9 1.7 convolution_bitcast_fusion
  261.1 99.8 %reduce-scatter.11.cloned.1.call-done = f32[16,256]{1,0:T(8,128)} async-done(((f32[512,256]{1,0:T(8,128)}), f32[16,256]{1,0:T(8,128)}) %reduce-scatter.11.cloned.1.call-update) | async-done | bytes 16400 | tf_op jit(solution)/shard_map/reduce_scatter | solution.py:52
  364.8 104.2 %reduce-scatter.9.cloned.1.call-done = f32[16,256]{1,0:T(8,128)} async-done(((f32[512,256]{1,0:T(8,128)}), f32[16,256]{1,0:T(8,128)}) %reduce-scatter.9.cloned.1.call-update) | async-done | bytes 16400 | tf_op jit(solution)/shard_map/reduce_scatter | solution.py:52
  469.0 72.4 %all-gather.10.cloned.1.call-done = f32[10,256,256]{2,1,0:T(8,128)} async-done(((f32[10,8,256]{2,1,0:T(8,128)}), f32[10,256,256]{2,1,0:T(8,128)}) %all-gather.10.cloned.1.call-update) | async-done | bytes 2621456 | tf_op jit(solution)/shard_map/all_gather | solution.py:89
  545.2 103.2 %reduce-scatter.7.cloned.1.call-done = f32[16,256]{1,0:T(8,128)} async-done(((f32[512,256]{1,0:T(8,128)}), f32[16,256]{1,0:T(8,128)}) %reduce-scatter.7.cloned.1.call-update) | async-done | bytes 16400 | tf_op jit(solution)/shard_map/reduce_scatter | solution.py:52
  654.2 102.5 %reduce-scatter.5.cloned.1.call-done = f32[16,256]{1,0:T(8,128)} async-done(((f32[512,256]{1,0:T(8,128)}), f32[16,256]{1,0:T(8,128)}) %reduce-scatter.5.cloned.1.call-update) | async-done | bytes 16400 | tf_op jit(solution)/shard_map/reduce_scatter | solution.py:52
  760.5 1.9 pad_maximum_fusion.2
  764.3 65.2 %all-gather.12.cloned.1.call-done = f32[10,256,256]{2,1,0:T(8,128)} async-done(((f32[10,8,256]{2,1,0:T(8,128)}), f32[10,256,256]{2,1,0:T(8,128)}) %all-gather.12.cloned.1.call-update) | async-done | bytes 2621456 | tf_op jit(solution)/shard_map/all_gather | solution.py:90
  829.5 417.1 %all-reduce.5.cloned.1.call-done = (f32[2,256,256]{2,1,0:T(8,128)}, f32[3,256,256]{2,1,0:T(8,128)}, f32[4,256,256]{2,1,0:T(8,128)}, f32[1,256,256]{2,1,0:T(8,128)}) async-done(((f32[2,256,256]{2,1,0:T(8,128)}, f32[3,256,256]{2,1,0:T(8,128)}, f32[4,256,256]{2,1,0:T(8,128)}, f32[1,256,256]{2,1,0:T(8,128)}), (f32[2,256,256]{2,1,0:T(8,128)}, f32[3,256,256]{2,1,0:T(8,128)}, f32[4,256,256]{2,1,0:T(8,128)}, ...) | async-done | bytes 2621456 | tf_op jit(solution)/shard_map/psum | solution.py:137
  1246.6 1.5 fusion.18
  1249.5 1.5 fusion.66
  1254.0 1.6 fusion.7
  1258.0 1.5 fusion.5
  1261.3 1.5 fusion.6
  1264.8 1.6 convolution_subtract_fusion.11
  1269.2 1.8 copy.38
  1271.0 1.5 fusion.1
  1272.5 1.5 fusion.2
  1279.8 1.6 convolution_subtract_fusion.6
  (162 shorter events, 56.1 us)
Async XLA Ops:
  8.0 242.9 %all-reduce.7.cloned.1.call-start = ((), (), s32[]{:S(2)}) async-start(), calls=%async_computation.12 | async-start | bytes 2097152 | tf_op jit(solution)/shard_map/psum | solution.py:13
  9.0 128.2 %copy-start.19 = (f32[2,1,256,1,1,256]{5,4,3,2,1,0:T(1,128)S(1)}, f32[2,1,256,1,1,256]{5,4,3,2,1,0:T(1,128)}, u32[]{:S(2)}) copy-start(f32[2,1,256,1,1,256]{5,4,3,2,1,0:T(1,128)} %param.6) | copy-start | bytes 1572868
  136.6 124.5 %all-gather.8.cloned.1.call-start = ((), (), s32[]{:S(2)}) async-start(), calls=%async_computation.8 | async-start | bytes 1081344 | tf_op jit(solution)/shard_map/all_gather | solution.py:91
  137.1 223.8 %reduce-scatter.11.cloned.1.call-start = ((), (), s32[]{:S(2)}) async-start(), calls=%async_computation.7 | async-start | bytes 540672 | tf_op jit(solution)/shard_map/reduce_scatter | solution.py:52
  250.9 5.5 copy-start.24
  253.7 215.4 %reduce-scatter.9.cloned.1.call-start = ((), (), s32[]{:S(2)}) async-start(), calls=%async_computation.6 | async-start | bytes 540672 | tf_op jit(solution)/shard_map/reduce_scatter | solution.py:52
  253.7 4.6 copy-start.23
  255.6 285.9 %all-gather.10.cloned.1.call-start = ((), (), s32[]{:S(2)}) async-start(), calls=%async_computation.9 | async-start | bytes 2703360 | tf_op jit(solution)/shard_map/all_gather | solution.py:89
  256.3 392.1 %reduce-scatter.7.cloned.1.call-start = ((), (), s32[]{:S(2)}) async-start(), calls=%async_computation.5 | async-start | bytes 540672 | tf_op jit(solution)/shard_map/reduce_scatter | solution.py:52
  256.4 4.6 copy-start.27
  257.0 3.9 copy-start.26
  258.2 498.6 %reduce-scatter.5.cloned.1.call-start = ((), (), s32[]{:S(2)}) async-start(), calls=%async_computation.4 | async-start | bytes 540672 | tf_op jit(solution)/shard_map/reduce_scatter | solution.py:52
  260.1 569.4 %all-gather.12.cloned.1.call-start = ((), (), s32[]{:S(2)}) async-start(), calls=%async_computation.10 | async-start | bytes 2703360 | tf_op jit(solution)/shard_map/all_gather | solution.py:90
  260.7 985.9 %all-reduce.5.cloned.1.call-start = ((), (), s32[]{:S(2)}) async-start(), calls=%async_computation.11 | async-start | bytes 5242880 | tf_op jit(solution)/shard_map/psum | solution.py:137
  541.4 215.3 %copy-start = (f32[10,256,256]{2,1,0:T(8,128)S(1)}, f32[10,256,256]{2,1,0:T(8,128)}, u32[]{:S(2)}) copy-start(f32[10,256,256]{2,1,0:T(8,128)} %all-gather.10.cloned.1.call-done) | copy-start | bytes 7864324
  1251.1 5.0 copy-start.1
  1258.0 5.4 copy-start.2
  1259.6 5.2 copy-start.20
  1261.3 5.7 copy-start.7
  1271.0 3.9 copy-start.3
  1271.0 4.3 copy-start.5
  1275.2 6.8 copy-start.14
  1276.7 4.7 copy-start.17
  1279.7 3.9 copy-start.13
  (13 other events, 35.4 us)
Sparse Core Ops, SparseCore 0:
  136.7 114.1 all-reduce.6
  763.6 482.9 all-reduce.4
Sparse Core Ops, SparseCore 1:
  139.2 67.6 all-gather.7
  253.7 107.1 reduce-scatter.10
  363.8 105.2 reduce-scatter.8
  471.2 70.2 all-gather.9
  544.2 104.1 reduce-scatter.6
  651.4 105.3 reduce-scatter.4
  758.8 70.6 all-gather.11
where the time goes:
time: 1300 us; the launch traced here: 1290 us
  waiting for transfers between devices  1080 us (83%)
  blocking collectives  125 us (10%)
  matrix products  53.2 us (4%)
  between operations  16.7 us (1%)
    psum x1, waiting for transfers between devices, per_device(): summed = lax.psum(local_gram, ('prow', 'pcol'))  417 us
    reduce_scatter x4, waiting for transfers between devices, reduce_one(): lax.psum_scatter(term(jnp.int32(0), lax.axis_size('pcol') * count), 'pcol...  410 us
    all_gather x4, blocking collectives, rows_one(): return lax.all_gather(piece, 'pcol', axis=1, tiled=True)  125 us
    psum x1, waiting for transfers between devices, from_root(): return lax.psum(jnp.where(mine, array, jnp.zeros_like(array)), axis)  114 us
    all_gather x1, waiting for transfers between devices, per_device(): lax.all_gather(factor_top, 'pcol', axis=1, tiled=True)  72.4 us
    all_gather x1, waiting for transfers between devices, per_device(): lax.all_gather(adjoint_top, 'pcol', axis=1, tiled=True)  65.2 us
    dot_general x30, matrix products, matmul(): jnp.dot(left, right, precision=HIGHEST, preferred_element_type=jnp.float32)  27.1 us
  transfers between devices with their start and end apart: 9, of which 8 were waited for; matrix products, arithmetic and copies ran while one was open for 2% of the time, Pallas kernels for 0%

commit v1 on v0

--- a/solution.py
+++ b/solution.py
@@ -2,6 +2,7 @@
 import jax.numpy as jnp
 from jax import lax
 from jax.sharding import PartitionSpec as P
+from jax.lax import all_to_all, axis_size
 
 NB = 256
 K = 4
@@ -85,9 +86,15 @@
     low_factor = factor_low.reshape(cycles, sub_rows, K * NB)
     low_adjoint = adjoint_low.reshape(local_rows, K, NB)
     columns = low_factor.reshape(local_rows, K, NB)
+
+    def raise_cubes(block_here, device_axis):
+        return jnp.concatenate(
+            all_to_all(jnp.stack(axis_size(device_axis) * [block_here], 0), device_axis, 0, 0), 1
+        )
+
     top_factor, top_adjoint, inverses = (
         lax.all_gather(factor_top, "pcol", axis=1, tiled=True),
-        lax.all_gather(adjoint_top, "pcol", axis=1, tiled=True),
+        raise_cubes(adjoint_top, "pcol"),
         lax.all_gather(diag_inverse, "pcol", axis=1, tiled=True),
     )
     lower_grads = [None] * K

time: 1300 us -> 1340 us (1.031)
  waiting for transfers between devices: 1080 us -> 1110 us
    all_gather x1 -> x0, waiting for transfers between devices: 65.2 us -> none  [per_device(): lax.all_gather(adjoint_top, 'pcol', axis=1, tiled=True)]
    psum x1, waiting for transfers between devices: 417 us -> 481 us  [per_device(): summed = lax.psum(local_gram, ('prow', 'pcol'))]
    reduce_scatter x4, waiting for transfers between devices: 410 us -> 444 us  [reduce_one(): lax.psum_scatter(term(jnp.int32(0), lax.axis_size('pcol') * count), 'pcol...]
  transfers between devices with their start and end apart: 9 -> 9, of which waited for: 8 -> 7; matrix products, arithmetic and copies ran while one was open for 2% -> 2% of each run, Pallas kernels for 0% -> 0%
where the time goes in v1:
time: 1340 us
  waiting for transfers between devices  1110 us (83%)
  blocking collectives  125 us (9%)
  matrix products  51.6 us (4%)
  between operations  16.9 us (1%)
    psum x1, waiting for transfers between devices, per_device(): summed = lax.psum(local_gram, ('prow', 'pcol'))  481 us
    reduce_scatter x4, waiting for transfers between devices, reduce_one(): lax.psum_scatter(term(jnp.int32(0), lax.axis_size('pcol') * count), 'pcol...  444 us
    all_gather x4, blocking collectives, rows_one(): return lax.all_gather(piece, 'pcol', axis=1, tiled=True)  125 us
    psum x1, waiting for transfers between devices, from_root(): return lax.psum(jnp.where(mine, array, jnp.zeros_like(array)), axis)  114 us
    all_gather x1, waiting for transfers between devices, per_device(): lax.all_gather(factor_top, 'pcol', axis=1, tiled=True)  72.8 us
    dot_general x30, matrix products, matmul(): jnp.dot(left, right, precision=HIGHEST, preferred_element_type=jnp.float32)  26.9 us
  transfers between devices with their start and end apart: 9, of which 7 were waited for; matrix products, arithmetic and copies ran while one was open for 2% of the time, Pallas kernels for 0%

profile of v1, /device:TPU:8, one launch (start us, length us, event | category | flops | bytes accessed | tf_op | source)
XLA Modules:
  0.0 1339.0 jit_solution(2556677705316282470)
XLA Ops:
  9.0 37.8 %all-gather.3 = f32[2,256,256]{2,1,0:T(8,128)S(1)} all-gather(f32[2,8,256]{2,1,0:T(8,128)S(1)} %get-tuple-element.15), channel_id=5, replica_groups=mesh['prow'=16,'pcol'=32] {'pcol'}, dimensions={1}, use_global_device_ids=true | all-gather | bytes 540672 | tf_op jit(solution)/shard_map/all_gather | solution.py:45
  46.8 28.5 %all-gather.2 = f32[2,256,256]{2,1,0:T(8,128)S(1)} all-gather(f32[2,8,256]{2,1,0:T(8,128)S(1)} %get-tuple-element.16), channel_id=4, replica_groups=mesh['prow'=16,'pcol'=32] {'pcol'}, dimensions={1}, use_global_device_ids=true | all-gather | bytes 540672 | tf_op jit(solution)/shard_map/all_gather | solution.py:45
  76.7 29.8 %all-gather.1 = f32[2,256,256]{2,1,0:T(8,128)S(1)} all-gather(f32[2,8,256]{2,1,0:T(8,128)S(1)} %get-tuple-element.17), channel_id=3, replica_groups=mesh['prow'=16,'pcol'=32] {'pcol'}, dimensions={1}, use_global_device_ids=true | all-gather | bytes 540672 | tf_op jit(solution)/shard_map/all_gather | solution.py:45
  107.3 28.5 %all-gather = f32[2,256,256]{2,1,0:T(8,128)S(1)} all-gather(f32[2,8,256]{2,1,0:T(8,128)S(1)} %get-tuple-element.14), channel_id=2, replica_groups=mesh['prow'=16,'pcol'=32] {'pcol'}, dimensions={1}, use_global_device_ids=true | all-gather | bytes 540672 | tf_op jit(solution)/shard_map/all_gather | solution.py:45
  137.2 113.6 %all-reduce.7.cloned.1.call-done = (f32[256,256]{1,0:T(8,128)}, f32[256,256]{1,0:T(8,128)}, f32[256,256]{1,0:T(8,128)}, f32[256,256]{1,0:T(8,128)}) async-done(((f32[256,256]{1,0:T(8,128)}, f32[256,256]{1,0:T(8,128)}, f32[256,256]{1,0:T(8,128)}, f32[256,256]{1,0:T(8,128)}), (f32[256,256]{1,0:T(8,128)}, f32[256,256]{1,0:T(8,128)}, f32[256,256]{1,0:T(8,128)}, ...) | async-done | bytes 1048592 | tf_op jit(solution)/shard_map/psum | solution.py:14
  250.8 1.6 convolution_bitcast_fusion
  256.2 1.8 stack.65
  258.0 12.8 all-to-all-start
  274.9 126.3 %reduce-scatter.11.cloned.1.call-done = f32[16,256]{1,0:T(8,128)} async-done(((f32[512,256]{1,0:T(8,128)}), f32[16,256]{1,0:T(8,128)}) %reduce-scatter.11.cloned.1.call-update) | async-done | bytes 16400 | tf_op jit(solution)/shard_map/reduce_scatter | solution.py:53
  405.2 112.0 %reduce-scatter.9.cloned.1.call-done = f32[16,256]{1,0:T(8,128)} async-done(((f32[512,256]{1,0:T(8,128)}), f32[16,256]{1,0:T(8,128)}) %reduce-scatter.9.cloned.1.call-update) | async-done | bytes 16400 | tf_op jit(solution)/shard_map/reduce_scatter | solution.py:53
  517.2 72.8 %all-gather.9.cloned.1.call-done = f32[10,256,256]{2,1,0:T(8,128)} async-done(((f32[10,8,256]{2,1,0:T(8,128)}), f32[10,256,256]{2,1,0:T(8,128)}) %all-gather.9.cloned.1.call-update) | async-done | bytes 2621456 | tf_op jit(solution)/shard_map/all_gather | solution.py:96
  593.4 103.8 %reduce-scatter.7.cloned.1.call-done = f32[16,256]{1,0:T(8,128)} async-done(((f32[512,256]{1,0:T(8,128)}), f32[16,256]{1,0:T(8,128)}) %reduce-scatter.7.cloned.1.call-update) | async-done | bytes 16400 | tf_op jit(solution)/shard_map/reduce_scatter | solution.py:53
  703.8 101.6 %reduce-scatter.5.cloned.1.call-done = f32[16,256]{1,0:T(8,128)} async-done(((f32[512,256]{1,0:T(8,128)}), f32[16,256]{1,0:T(8,128)}) %reduce-scatter.5.cloned.1.call-update) | async-done | bytes 16400 | tf_op jit(solution)/shard_map/reduce_scatter | solution.py:53
  810.0 480.7 %all-reduce.5.cloned.1.call-done = (f32[2,256,256]{2,1,0:T(8,128)}, f32[3,256,256]{2,1,0:T(8,128)}, f32[4,256,256]{2,1,0:T(8,128)}, f32[256,256]{1,0:T(8,128)}) async-done(((f32[2,256,256]{2,1,0:T(8,128)}, f32[3,256,256]{2,1,0:T(8,128)}, f32[4,256,256]{2,1,0:T(8,128)}, f32[256,256]{1,0:T(8,128)}), (f32[2,256,256]{2,1,0:T(8,128)}, f32[3,256,256]{2,1,0:T(8,128)}, f32[4,256,256]{2,1,0:T(8,128)}, ...) | async-done | bytes 2621456 | tf_op jit(solution)/shard_map/psum | solution.py:144
  1290.7 1.6 fusion.19
  1293.6 1.5 fusion.67
  1298.2 1.6 fusion.7
  1302.2 1.5 fusion.5
  1305.5 1.5 fusion.6
  1309.0 1.6 convolution_subtract_fusion.11
  1313.4 1.8 copy.56
  1315.2 1.5 fusion.1
  1316.7 1.5 fusion.2
  1324.0 1.6 convolution_subtract_fusion.6
  (165 shorter events, 54.5 us)
Async XLA Ops:
  8.0 242.8 %all-reduce.7.cloned.1.call-start = ((), (), s32[]{:S(2)}) async-start(), calls=%async_computation.12 | async-start | bytes 2097152 | tf_op jit(solution)/shard_map/psum | solution.py:14
  9.0 128.2 %copy-start.19 = (f32[2,1,256,1,1,256]{5,4,3,2,1,0:T(1,128)S(1)}, f32[2,1,256,1,1,256]{5,4,3,2,1,0:T(1,128)}, u32[]{:S(2)}) copy-start(f32[2,1,256,1,1,256]{5,4,3,2,1,0:T(1,128)} %param.6) | copy-start | bytes 1572868
  136.5 138.4 %all-gather.7.cloned.1.call-start = ((), (), s32[]{:S(2)}) async-start(), calls=%async_computation.9 | async-start | bytes 1081344 | tf_op jit(solution)/shard_map/all_gather | solution.py:98
  137.1 264.2 %reduce-scatter.11.cloned.1.call-start = ((), (), s32[]{:S(2)}) async-start(), calls=%async_computation.8 | async-start | bytes 540672 | tf_op jit(solution)/shard_map/reduce_scatter | solution.py:53
  250.8 5.4 copy-start.27
  253.6 263.6 %reduce-scatter.9.cloned.1.call-start = ((), (), s32[]{:S(2)}) async-start(), calls=%async_computation.7 | async-start | bytes 540672 | tf_op jit(solution)/shard_map/reduce_scatter | solution.py:53
  255.5 334.6 %all-gather.9.cloned.1.call-start = ((), (), s32[]{:S(2)}) async-start(), calls=%async_computation.10 | async-start | bytes 2703360 | tf_op jit(solution)/shard_map/all_gather | solution.py:96
  258.0 12.9 copy-start.24
  258.0 1032.7 %all-to-all-start = ((f32[32,10,8,256]{3,2,1,0:T(8,128)}), f32[32,10,8,256]{3,2,1,0:T(8,128)}, u32[]{:S(2)}, u32[]{:S(2)}) async-start(f32[32,10,8,256]{3,2,1,0:T(8,128)} %stack.65), calls=%async_computation.4 | async-start | bytes 5242880 | tf_op jit(solution)/shard_map/all_to_all | solution.py:92
  270.9 426.3 %reduce-scatter.7.cloned.1.call-start = ((), (), s32[]{:S(2)}) async-start(), calls=%async_computation.6 | async-start | bytes 540672 | tf_op jit(solution)/shard_map/reduce_scatter | solution.py:53
  272.7 532.7 %reduce-scatter.5.cloned.1.call-start = ((), (), s32[]{:S(2)}) async-start(), calls=%async_computation.5 | async-start | bytes 540672 | tf_op jit(solution)/shard_map/reduce_scatter | solution.py:53
  274.7 1016.0 %all-reduce.5.cloned.1.call-start = ((), (), s32[]{:S(2)}) async-start(), calls=%async_computation.11 | async-start | bytes 5242880 | tf_op jit(solution)/shard_map/psum | solution.py:144
  591.2 214.2 %copy-start = (f32[10,256,256]{2,1,0:T(8,128)S(1)}, f32[10,256,256]{2,1,0:T(8,128)}, u32[]{:S(2)}) copy-start(f32[10,256,256]{2,1,0:T(8,128)} %all-gather.9.cloned.1.call-done) | copy-start | bytes 7864324
  1295.3 5.0 copy-start.1
  1302.2 5.4 copy-start.2
  1303.8 5.2 copy-start.20
  1305.5 5.6 copy-start.7
  1315.2 3.9 copy-start.3
  1315.2 4.3 copy-start.5
  1319.4 6.8 copy-start.14
  1320.5 3.5 copy-start.22
  1320.9 4.7 copy-start.17
  1323.9 3.9 copy-start.13
  1327.4 3.3 copy-start.12
  (14 other events, 34.5 us)
Sparse Core Ops, SparseCore 0:
  136.6 114.1 all-reduce.6
  809.3 481.3 all-reduce.4
Sparse Core Ops, SparseCore 1:
  139.1 67.6 all-gather.6
  253.7 147.5 reduce-scatter.10
  404.1 113.0 reduce-scatter.8
  519.4 70.6 all-gather.8
  592.8 104.3 reduce-scatter.6
  700.3 105.1 reduce-scatter.4
